TPU v7x, 512 devices: a whole 4x4x16 slice. The times are simulated.
512 devices in a mesh: dp: 16 (over y, x), vocab: 32 (over z, core).
Axes of the slice: x: 4, y: 4, z: 16, core: 2. Of those that a mesh axis runs over, the one named last changes fastest.
Arguments:
- hidden: bfloat16 [16384, 5120], P('dp', 'vocab'), may hold values from -6 to 6
- logit_grad: bfloat16 [16384, 6144], P('dp', 'vocab'), may hold values from -0.3984375 to 0.3984375
- predict_mask: int32 [16384], P('dp'), may hold values 0 or 1
- slot_grads: bfloat16 [512, 32, 6, 5120], P(('dp', 'vocab')), may hold values from -6 to 6
- slot_rows: int32 [512, 32, 6], P(('dp', 'vocab')), may hold values from 0 to 191
- slot_counts: int32 [512, 32], P(('dp', 'vocab')), may hold values from 0 to 6, as said below
- master: float32 [6144, 5120], P(('vocab', 'dp')), may hold values from -0.1 to 0.1
- first_moment: float32 [6144, 5120], P(('vocab', 'dp')), may hold values from -2 to 2
- second_moment: float32 [6144, 5120], P(('vocab', 'dp')), may hold values from 0.5 to 8
Outputs:
- master_new: float32 [6144, 5120], P(('vocab', 'dp'))
- first_new: float32 [6144, 5120], P(('vocab', 'dp'))
- second_new: float32 [6144, 5120], P(('vocab', 'dp'))
- table_new: bfloat16 [6144, 5120], P('vocab')
Inputs may be any that keep to these rules, and one draw needn't show every extreme that they name: `slot_counts`: some owner receives 6 live slots from every sender, in every draw.
All inputs are finite; a program needn't handle non-finite values. No bound on the sum of `predict_mask` on one device may be relied on, other than what follows from the above.
Results may differ from a plain program's by a relative error of at most 0.0004.
Values may be sent and summed in bfloat16 or wider, within the bound.
A program may use at most 64 MiB of HBM per device.

v0:
```python
import jax
import jax.numpy as jnp
from jax import lax
from jax.sharding import PartitionSpec as P

STEP = 8


def local(
    hidden,
    logit_grad,
    predict_mask,
    slot_grads,
    slot_rows,
    slot_counts,
    master,
    first_moment,
    second_moment,
):
    masked = logit_grad * predict_mask.astype(jnp.bfloat16)[:, None]
    rows_block = logit_grad.shape[1]
    width = slot_grads.shape[3]
    contract = (((0,), (0,)), ((), ()))
    head_part = lax.dot_general(
        masked,
        lax.all_gather(hidden, "vocab", axis=1, tiled=True),
        contract,
        preferred_element_type=jnp.float32,
    )
    slot_index = jnp.arange(slot_grads.shape[2], dtype=jnp.int32)[None, None, :]
    alive_slot = slot_index < slot_counts[:, :, None]
    slot_ids = jnp.where(alive_slot, slot_rows, -1).astype(jnp.bfloat16)
    arrived, arrived_ids = (
        lax.all_to_all(slot_grads, "vocab", split_axis=1, concat_axis=0, tiled=True),
        lax.all_to_all(slot_ids, "vocab", split_axis=1, concat_axis=0, tiled=True),
    )
    arrived = arrived.reshape(-1, width)
    arrived_ids = arrived_ids.reshape(-1).astype(jnp.float32)
    row_labels = jnp.arange(rows_block, dtype=jnp.float32)[:, None]
    picked = (row_labels == arrived_ids[None, :]).astype(jnp.bfloat16)
    embed_part = jnp.dot(picked, arrived, preferred_element_type=jnp.float32)
    head_shard = lax.psum_scatter(head_part, "dp", scatter_dimension=0, tiled=True)
    embed_shard = lax.psum_scatter(embed_part, "dp", scatter_dimension=0, tiled=True)
    gradient = head_shard + embed_shard
    first_new = 0.9 * first_moment + 0.1 * gradient
    second_new = 0.95 * second_moment + 0.05 * gradient * gradient
    first_hat = first_new / (1.0 - 0.9**STEP)
    second_hat = second_new / (1.0 - 0.95**STEP)
    master_new = master - 0.05 * (first_hat / (jnp.sqrt(second_hat) + 1e-08) + 0.1 * master)
    table_new = lax.all_gather(master_new.astype(jnp.bfloat16), "dp", axis=0, tiled=True)
    return (master_new, first_new, second_new, table_new)


def solution(mesh):
    in_specs = (
        P("dp", "vocab"),
        P("dp", "vocab"),
        P("dp"),
        P(("dp", "vocab"), None, None, None),
        P(("dp", "vocab"), None, None),
        P(("dp", "vocab"), None),
        P(("vocab", "dp"), None),
        P(("vocab", "dp"), None),
        P(("vocab", "dp"), None),
    )
    out_specs = (
        P(("vocab", "dp"), None),
        P(("vocab", "dp"), None),
        P(("vocab", "dp"), None),
        P("vocab", None),
    )
    return jax.shard_map(local, mesh=mesh, in_specs=in_specs, out_specs=out_specs, check_vma=False)
```

profile of v0, /device:TPU:6, one launch (start us, length us, event | category | flops | bytes accessed | tf_op | source)
XLA Modules:
  0.0 406.2 jit_solution(3939633975617088747)
XLA Ops:
  7.2 0.0 all-gather.4.cloned.1.call-start
  7.2 0.7 all-gather.4.cloned.1.call-update
  7.9 0.8 copy.19
  8.7 1.4 fusion.6
  10.0 15.5 %all-to-all-start = ((bf16[1,32,6]{2,0,1:T(2,128)(2,1)}), bf16[1,32,6]{2,0,1:T(2,128)(2,1)S(1)}, u32[]{:S(2)}, u32[]{:S(2)}) async-start(bf16[1,32,6]{2,0,1:T(2,128)(2,1)} %fusion.6), calls=%async_computation | async-start | bytes 32768 | tf_op jit(solution)/shard_map/all_to_all | solution.py:35
  25.5 0.0 copy-start.7
  25.5 4.2 %copy.20 = bf16[1,32,6,5120]{3,2,0,1:T(8,128)(2,1)} copy(bf16[1,32,6,5120]{3,1,2,0:T(8,128)(2,1)} %param.12) | data formatting | bytes 3932160 | tf_op args[3]
  29.7 0.0 copy-start.1
  29.7 8.2 %all-to-all-done = bf16[1,32,6]{2,0,1:T(2,128)(2,1)S(1)} async-done(((bf16[1,32,6]{2,0,1:T(2,128)(2,1)}), bf16[1,32,6]{2,0,1:T(2,128)(2,1)S(1)}, u32[]{:S(2)}, u32[]{:S(2)}) %all-to-all-start) | async-done | bytes 416 | tf_op jit(solution)/shard_map/all_to_all | solution.py:35
  37.9 4.1 %all-to-all-start.1 = ((bf16[1,32,6,5120]{3,2,0,1:T(8,128)(2,1)}), bf16[1,32,6,5120]{3,2,0,1:T(8,128)(2,1)S(1)}, u32[]{:S(2)}, u32[]{:S(2)}) async-start(bf16[1,32,6,5120]{3,2,0,1:T(8,128)(2,1)} %copy.20), calls=%async_computation.1 | async-start | bytes 5242880 | tf_op jit(solution)/shard_map/all_to_all | solution.py:34
  42.1 0.0 all-gather.6.cloned.1.call-start
  42.1 0.0 copy-done.7
  42.1 0.1 convert_reduce_fusion
  42.2 0.1 reshape.68
  42.3 151.7 %all-to-all-done.1 = bf16[1,32,6,5120]{3,2,0,1:T(8,128)(2,1)S(1)} async-done(((bf16[1,32,6,5120]{3,2,0,1:T(8,128)(2,1)}), bf16[1,32,6,5120]{3,2,0,1:T(8,128)(2,1)S(1)}, u32[]{:S(2)}, u32[]{:S(2)}) %all-to-all-start.1) | async-done | bytes 1966112 | tf_op jit(solution)/shard_map/all_to_all | solution.py:34
  194.0 2.1 reshape.67
  196.0 0.0 copy-start
  196.0 9.6 %all-gather.4.cloned.1.call-done = bf16[1024,5120]{0,1:T(8,128)(2,1)} async-done(((bf16[1024,160]{0,1:T(8,128)(2,1)}), bf16[1024,5120]{0,1:T(8,128)(2,1)}) %all-gather.4.cloned.1.call-update) | async-done | bytes 10485776 | tf_op jit(solution)/shard_map/all_gather | solution.py:26
  205.6 0.0 copy-done.1
  205.7 7.6 %fusion.1 = f32[192,5120]{1,0:T(8,128)S(1)} fusion(bf16[1024,5120]{0,1:T(8,128)(2,1)} %all-gather.4.cloned.1.call-done, bf16[1024,192]{0,1:T(8,128)(2,1)S(1)} %copy-done.1, bf16[1024]{0:T(1024)(128)(2,1)S(1)} %convert_element_type.20), kind=kOutput, calls=%fused_computation.2 | convolution fusion | flops 2013462528 | bytes 14813184 | tf_op jit(solution)/shard_map/dot_general | solution.py:24
  213.2 0.0 copy-done
  213.2 2.6 convolution_add_fusion
  215.8 0.0 copy-start.2
  215.8 0.0 copy-start.3
  215.8 0.0 copy-start.4
  215.8 77.9 %fusion = f32[16,5120]{1,0:T(8,128)S(1)} fusion(f32[192,5120]{1,0:T(8,128)} %convolution_add_fusion), kind=kCustom, calls=%all-reduce-scatter | all-reduce-scatter fusion | flops 1310721 | bytes 4261888
  293.7 3.2 collective-permute-start.2
  296.9 3.7 collective-permute-start.1
  300.6 4.3 %collective-permute-start = (f32[16,5120]{1,0:T(8,128)S(1)}, f32[16,5120]{1,0:T(8,128)}, u32[]{:S(2)}, u32[]{:S(2)}) collective-permute-start(f32[16,5120]{1,0:T(8,128)S(1)} %fusion), channel_id=1, source_target_pairs={{0,32},{32,64},{64,96},{96,128},{128,160},{160,192},{192,224},{224... | collective-permute-start | bytes 983048
  305.0 2.4 collective-permute-start.3
  307.3 1.3 dynamic-slice.4
  309.3 2.6 collective-permute-done.3
  311.9 0.0 copy-start.6
  311.9 0.0 collective-permute-done.2
  311.9 0.5 collective-permute-done.1
  312.4 0.2 copy-done.6
  312.6 0.0 copy-start.5
  312.6 0.7 copy-done.5
  313.3 2.6 collective-permute-done
  315.9 5.8 %concatenate = f32[76,5120]{1,0:T(8,128)S(1)} concatenate(f32[12,5120]{1,0:T(8,128)} %copy-done.6, f32[16,5120]{1,0:T(8,128)S(1)} %collective-permute-done.2, f32[16,5120]{1,0:T(8,128)} %copy-done.5, f32[16,5120]{1,0:T(8,128)} %collective-permute-done, f32[16,5120]{1,0:T(8,128)S(1)} %fusion), dimensions={0} | concatenate | bytes 3112960
  321.8 0.0 copy-done.2
  321.8 0.0 copy-done.3
  321.8 0.0 copy-done.4
  321.8 1.2 convert_bitcast_fusion
  323.0 0.0 all-gather.6.cloned.1.call-update
  323.0 72.4 %all-gather.6.cloned.1.call-done = bf16[16,12,5120]{2,1,0:T(8,128)(2,1)} async-done(((bf16[1,12,5120]{2,1,0:T(8,128)(2,1)}), bf16[16,12,5120]{2,1,0:T(8,128)(2,1)}) %all-gather.6.cloned.1.call-update) | async-done | bytes 1966096 | tf_op jit(solution)/shard_map/all_gather | solution.py:50
  395.4 4.0 reshape.70
  (2 shorter events, 0.0 us)
Async XLA Ops:
  7.2 198.5 %all-gather.4.cloned.1.call-start = ((), (), s32[]{:S(2)}) async-start(), calls=%async_computation.2 | async-start | bytes 10813440 | tf_op jit(solution)/shard_map/all_gather | solution.py:26
  10.0 27.9 %all-to-all-start = ((bf16[1,32,6]{2,0,1:T(2,128)(2,1)}), bf16[1,32,6]{2,0,1:T(2,128)(2,1)S(1)}, u32[]{:S(2)}, u32[]{:S(2)}) async-start(bf16[1,32,6]{2,0,1:T(2,128)(2,1)} %fusion.6), calls=%async_computation | async-start | bytes 32768 | tf_op jit(solution)/shard_map/all_to_all | solution.py:35
  25.5 16.6 %copy-start.7 = (s32[1024]{0:T(1024)S(1)}, s32[1024]{0:T(1024)}, u32[]{:S(2)}) copy-start(s32[1024]{0:T(1024)} %param.11) | copy-start | bytes 12292
  29.7 175.9 %copy-start.1 = (bf16[1024,192]{0,1:T(8,128)(2,1)S(1)}, bf16[1024,192]{0,1:T(8,128)(2,1)}, u32[]{:S(2)}) copy-start(bf16[1024,192]{0,1:T(8,128)(2,1)} %param.10) | copy-start | bytes 1179652
  37.9 156.0 %all-to-all-start.1 = ((bf16[1,32,6,5120]{3,2,0,1:T(8,128)(2,1)}), bf16[1,32,6,5120]{3,2,0,1:T(8,128)(2,1)S(1)}, u32[]{:S(2)}, u32[]{:S(2)}) async-start(bf16[1,32,6,5120]{3,2,0,1:T(8,128)(2,1)} %copy.20), calls=%async_computation.1 | async-start | bytes 5242880 | tf_op jit(solution)/shard_map/all_to_all | solution.py:34
  42.1 353.3 %all-gather.6.cloned.1.call-start = ((), (), s32[]{:S(2)}) async-start(), calls=%async_computation.3 | async-start | bytes 2785280 | tf_op jit(solution)/shard_map/all_gather | solution.py:50
  196.0 17.2 %copy-start = (bf16[192,5120]{1,0:T(8,128)(2,1)S(1)}, bf16[192,5120]{1,0:T(8,128)(2,1)}, u32[]{:S(2)}) copy-start(bf16[192,5120]{1,0:T(8,128)(2,1)} %reshape.67) | copy-start | bytes 5898244
  215.8 106.0 %copy-start.2 = (f32[12,5120]{1,0:T(8,128)S(1)}, f32[12,5120]{1,0:T(8,128)}, u32[]{:S(2)}) copy-start(f32[12,5120]{1,0:T(8,128)} %param.15) | copy-start | bytes 737284
  215.8 106.0 %copy-start.3 = (f32[12,5120]{1,0:T(8,128)S(1)}, f32[12,5120]{1,0:T(8,128)}, u32[]{:S(2)}) copy-start(f32[12,5120]{1,0:T(8,128)} %param.16) | copy-start | bytes 737284
  215.8 106.0 %copy-start.4 = (f32[12,5120]{1,0:T(8,128)S(1)}, f32[12,5120]{1,0:T(8,128)}, u32[]{:S(2)}) copy-start(f32[12,5120]{1,0:T(8,128)} %param.17) | copy-start | bytes 737284
  293.7 18.2 %collective-permute-start.2 = (f32[16,5120]{1,0:T(8,128)S(1)}, f32[16,5120]{1,0:T(8,128)S(1)}, u32[]{:S(2)}, u32[]{:S(2)}) collective-permute-start(f32[16,5120]{1,0:T(8,128)S(1)} %fusion), channel_id=1, source_target_pairs={{0,96},{32,128},{64,160},{96,192},{128,224},{160,256},{192,288},{2... | collective-permute-start | bytes 983048
  296.9 15.4 %collective-permute-start.1 = (f32[16,5120]{1,0:T(8,128)S(1)}, f32[16,5120]{1,0:T(8,128)S(1)}, u32[]{:S(2)}, u32[]{:S(2)}) collective-permute-start(f32[16,5120]{1,0:T(8,128)S(1)} %fusion), channel_id=1, source_target_pairs={{0,64},{32,96},{64,128},{96,160},{128,192},{160,224},{192,256},{22... | collective-permute-start | bytes 983048
  300.6 15.3 %collective-permute-start = (f32[16,5120]{1,0:T(8,128)S(1)}, f32[16,5120]{1,0:T(8,128)}, u32[]{:S(2)}, u32[]{:S(2)}) collective-permute-start(f32[16,5120]{1,0:T(8,128)S(1)} %fusion), channel_id=1, source_target_pairs={{0,32},{32,64},{64,96},{96,128},{128,160},{160,192},{192,224},{224... | collective-permute-start | bytes 983048
  305.0 6.9 %collective-permute-start.3 = (f32[12,5120]{1,0:T(8,128)S(1)}, f32[12,5120]{1,0:T(8,128)S(1)}, u32[]{:S(2)}, u32[]{:S(2)}) collective-permute-start(f32[12,5120]{1,0:T(8,128)S(1)} %slice), channel_id=1, source_target_pairs={{0,128},{32,160},{64,192},{96,224},{128,256},{160,288},{192,320},{... | collective-permute-start | bytes 737288
  311.9 0.7 copy-start.6
  312.6 0.7 copy-start.5
Sparse Core Ops, SparseCore 0:
  10.1 195.4 all-gather.3
  323.1 72.1 all-gather.5
where the time goes:
time: 408 us; the launch traced here: 406 us
  waiting for transfers between devices  248 us (61%)
  blocking collectives  77.9 us (19%)
  starting transfers between devices  33.2 us (8%)
  local copies, waits for them, and re-layouts  19.3 us (5%)
  between operations  14.8 us (4%)
  matrix products  10.2 us (2%)
    all_to_all x1, waiting for transfers between devices, local(): lax.all_to_all(slot_grads, 'vocab', split_axis=1, concat_axis=0, tiled=True)  152 us
    unnamed x1, blocking collectives  77.9 us
    all_gather x1, waiting for transfers between devices, local(): lax.all_gather(master_new.astype(jnp.bfloat16), 'dp', axis=0, tiled=True)  72.4 us
    unnamed x22, local copies, waits for them, and re-layouts  17.1 us
    all_to_all x1, starting transfers between devices, local(): lax.all_to_all(slot_ids, 'vocab', split_axis=1, concat_axis=0, tiled=True)  15.5 us
    unnamed x4, starting transfers between devices  13.5 us
    all_gather x1, waiting for transfers between devices, local(): lax.all_gather(hidden, 'vocab', axis=1, tiled=True)  9.61 us
    all_to_all x1, waiting for transfers between devices, local(): lax.all_to_all(slot_ids, 'vocab', split_axis=1, concat_axis=0, tiled=True)  8.17 us
  transfers between devices with their start and end apart: 8, of which 7 were waited for; matrix products, arithmetic and copies ran while one was open for 2% of the time, Pallas kernels for 0%

commit v1 on v0

v1 whole, which is shorter than its diff:
```python
import jax
import jax.numpy as jnp
from jax import lax
from jax.experimental import pallas as pl
from jax.experimental.pallas import tpu as pltpu
from jax.sharding import PartitionSpec as P

STEP = 8
Z = 16
NX = 4
NY = 4
DP = NX * NY
COLS = 640
NB = 8
UNITS = 48
PARTS = 4
PU = UNITS // PARTS
MESH = pl.DeviceIdType.MESH
F32 = jnp.float32
BF16 = jnp.bfloat16


def kernel(
    hid, logit, mask, slots, ids, master, first, second,
    master_o, first_o, second_o, table,
    hall, masked, outbox, inbox, part, ring, head, r1, q, r2, grad, emb,
    ag_s, ag_r, sib_s, sib_r, sl_s, sl_r, z_s, z_r,
    r1_s, r1_r, r2_s, r2_r, e_s, e_r, t1_s, t1_r, t2_s, t2_r, loc,
):
    d = lax.axis_index("dp")
    v = lax.axis_index("vocab")
    z, c = v // 2, v % 2
    y, x = d // NX, d % NX
    pg, h = d // 2, d % 2
    me = d * 2 + c

    def rc(src, dst, ss, rs, dev):
        return pltpu.make_async_remote_copy(
            src_ref=src, dst_ref=dst, send_sem=ss, recv_sem=rs,
            device_id=dev, device_id_type=MESH)

    up = (d, (v + 2) % 32)
    down = (d, (v + 30) % 32)
    sib = (d, z * 2 + (1 - c))
    zdir = (d, (v + 2 + 28 * c) % 32)

    bar = pltpu.get_barrier_semaphore()
    pl.semaphore_signal(bar, inc=1, device_id=up, device_id_type=MESH)
    pl.semaphore_signal(bar, inc=1, device_id=down, device_id_type=MESH)

    def greet(k, carry):
        o = (me + k) % 32
        pl.semaphore_signal(bar, inc=1, device_id=(o // 2, z * 2 + o % 2), device_id_type=MESH)
        return carry

    lax.fori_loop(1, 32, greet, 0)
    pl.semaphore_wait(bar, 33)

    def plane_at(sg, s):
        return (z - s + 16) % 16 if sg == 0 else (z + s) % 16

    def ag(sg, s, half):
        idx = plane_at(sg, s - 1) * 2 + c
        rows = pl.ds(80 * half, 80)
        ref = hall.at[idx, rows]
        src = hid.at[rows] if s == 1 else ref
        return rc(src, ref, ag_s.at[sg, s, half], ag_r.at[sg, s, half], up if sg == 0 else down)

    def ag_arrival(sg, s, half):
        idx = plane_at(sg, s) * 2 + c
        ref = hall.at[idx, pl.ds(80 * half, 80)]
        rc(ref, ref, ag_s.at[sg, s, half], ag_r.at[sg, s, half], up).wait_recv()

    def share(sg, s, half):
        idx = plane_at(sg, s) * 2 + c
        ref = hall.at[idx, pl.ds(80 * half, 80)]
        return rc(ref, ref, sib_s.at[sg, s, half], sib_r.at[sg, s, half], sib)

    def share_arrival(sg, s, half):
        idx = plane_at(sg, s) * 2 + 1 - c
        ref = hall.at[idx, pl.ds(80 * half, 80)]
        rc(ref, ref, sib_s.at[sg, s, half], sib_r.at[sg, s, half], sib).wait_recv()

    own_share = rc(hid, hall.at[v], sib_s.at[0, 0, 0], sib_r.at[0, 0, 0], sib)
    for half in (0, 1):
        ag(0, 1, half).start()
        ag(1, 1, half).start()
    own_share.start()
    own_copy = pltpu.make_async_copy(hid, hall.at[v], loc.at[0])
    own_copy.start()

    r = lax.broadcasted_iota(jnp.int32, (256, 224), 0)
    k = lax.broadcasted_iota(jnp.int32, (256, 224), 1)
    e = r % 8
    i = (r // 8) % 8
    to_plane = jnp.where((r // 64) % 2 == 0, z + 24 - i, z + 9 + i) % 16
    owner = to_plane * 2 + r // 128
    want = jnp.where(e < 6, e * 32 + owner, jnp.where(e == 6, 192 + owner, -1))
    select = jnp.where(want == k, 1.0, 0.0).astype(BF16)

    def slot_copy(g, w):
        to = (2 * g + w // 2, z * 2 + w % 2)
        return rc(outbox.at[g, w], inbox.at[me], sl_s.at[g * 4 + w], sl_r.at[me], to)

    def send_slots(g, carry):
        cols = pl.ds(pl.multiple_of(g * COLS, 128), COLS)
        rows = jnp.dot(select[:, :192], slots[:, cols], preferred_element_type=F32)
        rows = rows + jnp.dot(select[:, 192:], ids[...], preferred_element_type=F32)
        outbox[g] = rows.astype(BF16).reshape(4, 64, COLS)
        for w in range(4):
            mine = (2 * g + w // 2 == d) & (w % 2 == c)

            @pl.when(mine)
            def _():
                pltpu.make_async_copy(outbox.at[g, w], inbox.at[me], sl_r.at[me]).start()

            @pl.when(jnp.logical_not(mine))
            def _():
                slot_copy(g, w).start()
        return carry

    lax.fori_loop(0, NB, send_slots, 0)
    masked[...] = logit[...] * mask[...].astype(BF16)

    kz = z // 2

    def block_of(n):
        t = (n + 1) // 2
        return (kz + 16 + jnp.where(n % 2 == 1, -t, t)) % NB

    def stage1(n, g, xfirst):
        if xfirst:
            return rc(head.at[n, :, g], r1.at[n, x], r1_s.at[n, g], r1_r.at[n, x], (y * NX + g, v))
        return rc(head.at[n, g], r1.at[n, y], r1_s.at[n, g], r1_r.at[n, y], (g * NX + x, v))

    def stage2(n, g, xfirst):
        if xfirst:
            return rc(q.at[n, g], r2.at[n, y], r2_s.at[n, g], r2_r.at[n, y], (g * NX + x, v))
        return rc(q.at[n, g], r2.at[n, x], r2_s.at[n, g], r2_r.at[n, x], (y * NX + g, v))

    def head_block(n, xfirst):
        kb = block_of(n)
        rows = hall[pl.ds(4 * kb, 4)].reshape(COLS, 1024)
        val = lax.dot_general(masked[...], rows, (((1,), (1,)), ((), ())), preferred_element_type=F32)
        head[n] = val.reshape(NY, NX, 3, 4, COLS)
        mine = x if xfirst else y
        for o in range(1, 4):
            stage1(n, (mine + o) % 4, xfirst).start()

    def head_mid(n, xfirst):
        mine = x if xfirst else y
        for o in range(1, 4):
            src = (mine + o) % 4
            ref = r1.at[n, src]
            rc(ref, ref, r1_s.at[n, src], r1_r.at[n, src], up).wait_recv()
        own = head[n, :, x] if xfirst else head[n, y]
        q[n] = own + r1[n, (mine + 1) % 4] + r1[n, (mine + 2) % 4] + r1[n, (mine + 3) % 4]
        then = y if xfirst else x
        for o in range(1, 4):
            stage2(n, (then + o) % 4, xfirst).start()

    def head_end(n, xfirst):
        then = y if xfirst else x
        for o in range(1, 4):
            src = (then + o) % 4
            ref = r2.at[n, src]
            rc(ref, ref, r2_s.at[n, src], r2_r.at[n, src], up).wait_recv()
        grad[block_of(n)] = (
            q[n, then] + r2[n, (then + 1) % 4] + r2[n, (then + 2) % 4] + r2[n, (then + 3) % 4]
        )

    def ag_step(s):
        for half in (0, 1):
            for sg in (0, 1):
                if s == 8 and half != sg:
                    continue
                ag_arrival(sg, s, half)
                if s < 7 or (s == 7 and half == sg):
                    ag(sg, s + 1, half).start()
                share(sg, s, half).start()

    def shares_of(s):
        for half in (0, 1):
            for sg in (0, 1):
                if s == 8 and half != sg:
                    continue
                share_arrival(sg, s, half)

    def embed_parts():
        def arrived(s, carry):
            rc(inbox.at[s], inbox.at[s], sl_s.at[s], sl_r.at[s], up).wait_recv()
            return carry

        lax.fori_loop(0, 32, arrived, 0)

        def pair(p, carry):
            rows = inbox[:, pl.ds(pl.multiple_of(16 * p, 16), 16), :]
            tags = rows[:, :, :512].astype(F32)
            sub = lax.broadcasted_iota(jnp.int32, (32, 16, 512), 1)
            tags = jnp.where(sub % 8 == 6, tags, 0.0)
            tags = jnp.sum(jnp.sum(tags, axis=0), axis=0, keepdims=True)
            lane = lax.broadcasted_iota(jnp.int32, (1, 512), 1)
            shift = jnp.where((lane // 8) % 2 == 1, 192.0, 0.0)
            tags = jnp.where(tags > 0.5, tags + shift, 0.0)
            row = lax.broadcasted_iota(jnp.int32, (384, 512), 0).astype(F32) + 1.0
            hot = jnp.where(row == tags, 1.0, 0.0).astype(BF16)
            val = jnp.dot(hot, rows.reshape(512, COLS), preferred_element_type=F32)
            part[pl.ds(2 * p, 2)] = val.reshape(2, UNITS, 4, COLS)
            return carry

        lax.fori_loop(0, 4, pair, 0)

    def z_copy(s, src, p):
        rows = pl.ds(p * PU, PU)
        return rc(src.at[rows], ring.at[s, rows], z_s.at[s, p], z_r.at[s, p], zdir)

    def z_arrival(s, p):
        ref = ring.at[s, pl.ds(p * PU, PU)]
        rc(ref, ref, z_s.at[s, p], z_r.at[s, p], zdir).wait_recv()

    def z_step(s):
        for p in range(PARTS):
            if s == 0:
                z_copy(0, part.at[0], p).start()
                continue
            z_arrival(s - 1, p)
            rows = pl.ds(p * PU, PU)
            ring[s - 1, rows] = ring[s - 1, rows] + part[s, rows]
            if s < 7:
                z_copy(s, ring.at[s - 1], p).start()
            else:

                @pl.when(c == 0)
                def _():
                    z_copy(s, ring.at[s - 1], p).start()

    own_copy.wait()
    ag_step(1)
    ag_step(2)
    own_idx = v + 1 - 2 * c
    rc(hid, hall.at[own_idx], sib_s.at[0, 0, 0], sib_r.at[0, 0, 0], sib).wait_recv()
    shares_of(1)
    head_block(0, True)
    ag_step(3)
    shares_of(2)
    shares_of(3)
    head_block(1, False)
    ag_step(4)
    head_block(2, True)
    head_mid(0, True)
    ag_step(5)
    shares_of(4)
    shares_of(5)
    head_block(3, False)
    ag_step(6)
    head_block(4, True)
    embed_parts()
    ag_step(7)
    z_step(0)
    head_mid(1, False)
    head_mid(2, True)
    ag_step(8)
    shares_of(6)
    shares_of(7)
    z_step(1)
    head_block(5, False)
    z_step(2)
    head_block(6, True)
    z_step(3)
    shares_of(8)
    head_block(7, False)
    z_step(4)
    head_mid(3, False)
    head_mid(4, True)
    z_step(5)
    head_mid(5, False)
    head_mid(6, True)
    z_step(6)
    head_mid(7, False)
    for n in range(5):
        head_end(n, n % 2 == 0)
    z_step(7)
    for n in range(5, 8):
        head_end(n, n % 2 == 0)

    fin = 7 - c

    def e_copy(t):
        return rc(ring.at[fin, pl.ds(3 * t, 3)], emb.at[c, pg], e_s.at[t], e_r.at[c, pg], (t, z * 2 + h))

    for p in range(PARTS):

        @pl.when(c == 0)
        def _():
            z_arrival(7, p)

        for t in range(4 * p, 4 * p + 4):
            mine = (t == d) & (h == c)

            @pl.when(mine)
            def _():
                pltpu.make_async_copy(
                    ring.at[fin, pl.ds(3 * t, 3)], emb.at[c, pg], e_r.at[c, pg]).start()

            @pl.when(jnp.logical_not(mine))
            def _():
                e_copy(t).start()

    corr1 = 1.0 / (1.0 - 0.9**STEP)
    corr2 = 1.0 / (1.0 - 0.95**STEP)
    for b in range(NB):
        for w in (0, 1):
            ref = emb.at[w, b]
            rc(ref, ref, e_s.at[b], e_r.at[w, b], up).wait_recv()
        g = grad[b] + emb[0, b] + emb[1, b]
        g = jnp.concatenate([g[0], g[1], g[2]], axis=0)
        cols = pl.ds(b * COLS, COLS)
        m = master[:, cols]
        fn = 0.9 * first[:, cols] + 0.1 * g
        sn = 0.95 * second[:, cols] + 0.05 * g * g
        mn = m - 0.05 * (fn * corr1 / (jnp.sqrt(sn * corr2) + 1e-08) + 0.1 * m)
        first_o[:, cols] = fn
        second_o[:, cols] = sn
        master_o[:, cols] = mn
        table[y, x, b // 4, :, pl.ds((b % 4) * COLS, COLS)] = mn.astype(BF16)

    def t1(w, g):
        ref = table.at[y, x, w]
        to = (y * NX + g, v) if w == 0 else (g * NX + x, v)
        return rc(ref, ref, t1_s.at[w, g], t1_r.at[w, x if w == 0 else y], to)

    def t1_arrival(w, g):
        ref = table.at[y, g, w] if w == 0 else table.at[g, x, w]
        rc(ref, ref, t1_s.at[w, g], t1_r.at[w, g], up).wait_recv()

    def t2(w, g):
        if w == 0:
            ref, to, i = table.at[y, :, w], (g * NX + x, v), y
        else:
            ref, to, i = table.at[:, x, w], (y * NX + g, v), x
        return rc(ref, ref, t2_s.at[w, g], t2_r.at[w, i], to)

    def t2_arrival(w, g):
        ref = table.at[g, :, w] if w == 0 else table.at[:, g, w]
        rc(ref, ref, t2_s.at[w, g], t2_r.at[w, g], up).wait_recv()

    firsts = (x, y)
    seconds = (y, x)
    for o in range(1, 4):
        for w in (0, 1):
            t1(w, (firsts[w] + o) % 4).start()
    for w in (0, 1):
        for o in range(1, 4):
            t1_arrival(w, (firsts[w] + o) % 4)
        for o in range(1, 4):
            t2(w, (seconds[w] + o) % 4).start()
    for w in (0, 1):
        for o in range(1, 4):
            t2_arrival(w, (seconds[w] + o) % 4)

    own_share.wait_send()
    for s in range(1, 9):
        for half in (0, 1):
            for sg in (0, 1):
                if s == 8 and half != sg:
                    continue
                ag(sg, s, half).wait_send()
                share(sg, s, half).wait_send()

    def slots_left(g, carry):
        for w in range(4):

            @pl.when(jnp.logical_not((2 * g + w // 2 == d) & (w % 2 == c)))
            def _():
                slot_copy(g, w).wait_send()
        return carry

    lax.fori_loop(0, NB, slots_left, 0)
    for n in range(NB):
        xfirst = n % 2 == 0
        for o in range(1, 4):
            stage1(n, ((x if xfirst else y) + o) % 4, xfirst).wait_send()
            stage2(n, ((y if xfirst else x) + o) % 4, xfirst).wait_send()
    for s in range(8):
        for p in range(PARTS):
            src = part.at[0] if s == 0 else ring.at[s - 1]
            if s < 7:
                z_copy(s, src, p).wait_send()
            else:

                @pl.when(c == 0)
                def _():
                    z_copy(s, src, p).wait_send()
    for t in range(DP):

        @pl.when(jnp.logical_not((t == d) & (h == c)))
        def _():
            e_copy(t).wait_send()
    for w in (0, 1):
        for o in range(1, 4):
            t1(w, (firsts[w] + o) % 4).wait_send()
            t2(w, (seconds[w] + o) % 4).wait_send()


def local(hidden, logit_grad, predict_mask, slot_grads, slot_rows, slot_counts, master, first, second):
    me = lax.axis_index("dp") * 2 + lax.axis_index("vocab") % 2
    live = jnp.arange(6, dtype=jnp.int32)[None, :] < slot_counts[0][:, None]
    tag = jnp.where(live, slot_rows[0] + 1, 0).astype(BF16)
    lane = jnp.arange(COLS, dtype=jnp.int32)
    wide = jnp.pad(tag, ((0, 0), (0, 2)))
    wide = jnp.tile(wide, (1, COLS // 8))
    ids = jnp.where((lane // 16 == me)[None, :], wide, jnp.zeros((), BF16))
    z = lax.axis_index("vocab") // 2
    plane = jnp.arange(32, dtype=jnp.int32) // 2
    rel = (plane - z - 1) % 16
    step = jnp.where(rel < 8, 7 - rel, rel - 8)
    ids = jnp.where((lane[None, :] // 8) % 2 == (step % 2)[:, None], ids, jnp.zeros((), BF16))
    slots = slot_grads[0].transpose(1, 0, 2).reshape(192, 5120)
    vm = pl.BlockSpec(memory_space=pltpu.VMEM)
    dma = pltpu.SemaphoreType.DMA
    out = pl.pallas_call(
        kernel,
        out_shape=(
            jax.ShapeDtypeStruct((12, 5120), F32),
            jax.ShapeDtypeStruct((12, 5120), F32),
            jax.ShapeDtypeStruct((12, 5120), F32),
            jax.ShapeDtypeStruct((NY, NX, 2, 12, 2560), BF16),
        ),
        in_specs=[vm] * 8,
        out_specs=(vm,) * 4,
        scratch_shapes=[
            pltpu.VMEM((32, 160, 1024), BF16),
            pltpu.VMEM((192, 1024), BF16),
            pltpu.VMEM((NB, 4, 64, COLS), BF16),
            pltpu.VMEM((32, 64, COLS), BF16),
            pltpu.VMEM((8, UNITS, 4, COLS), F32),
            pltpu.VMEM((8, UNITS, 4, COLS), F32),
            pltpu.VMEM((NB, NY, NX, 3, 4, COLS), F32),
            pltpu.VMEM((NB, 4, 4, 3, 4, COLS), F32),
            pltpu.VMEM((NB, 4, 3, 4, COLS), F32),
            pltpu.VMEM((NB, 4, 3, 4, COLS), F32),
            pltpu.VMEM((NB, 3, 4, COLS), F32),
            pltpu.VMEM((2, NB, 3, 4, COLS), F32),
            dma((2, 9, 2)), dma((2, 9, 2)), dma((2, 9, 2)), dma((2, 9, 2)),
            dma((32,)), dma((32,)), dma((8, PARTS)), dma((8, PARTS)),
            dma((NB, 4)), dma((NB, 4)), dma((NB, 4)), dma((NB, 4)),
            dma((DP,)), dma((2, NB)),
            dma((2, 4)), dma((2, 4)), dma((2, 4)), dma((2, 4)),
            dma((1,)),
        ],
        compiler_params=pltpu.CompilerParams(
            collective_id=0, has_side_effects=True, vmem_limit_bytes=60 * 1024 * 1024),
    )(hidden.T, logit_grad.T, predict_mask[None, :], slots, ids, master, first, second)
    table = out[3].transpose(0, 1, 3, 2, 4).reshape(192, 5120)
    return out[0], out[1], out[2], table


def solution(mesh):
    in_specs = (
        P("dp", "vocab"),
        P("dp", "vocab"),
        P("dp"),
        P(("dp", "vocab"), None, None, None),
        P(("dp", "vocab"), None, None),
        P(("dp", "vocab"), None),
        P(("vocab", "dp"), None),
        P(("vocab", "dp"), None),
        P(("vocab", "dp"), None),
    )
    out_specs = (
        P(("vocab", "dp"), None),
        P(("vocab", "dp"), None),
        P(("vocab", "dp"), None),
        P("vocab", None),
    )
    return jax.shard_map(local, mesh=mesh, in_specs=in_specs, out_specs=out_specs, check_vma=False)
```

time: 408 us -> 181 us (0.44)
  waiting for transfers between devices: 248 us -> 0 us
  Pallas kernels: 0 us -> 171 us
  blocking collectives: 77.9 us -> 0 us
  starting transfers between devices: 33.2 us -> 0 us
  between operations: 14.8 us -> 0.71 us
  local copies, waits for them, and re-layouts: 19.3 us -> 7.62 us
  matrix products: 10.2 us -> 0 us
    pallas_call x0 -> x1, Pallas kernels: none -> 171 us  [local(): pl.pallas_call(kernel, out_shape=(jax.ShapeDtypeStruct((12, 5120), F32),...]
    all_to_all x2 -> x0, waiting for transfers between devices: 160 us -> none  [the longest x1 152 us: local(): lax.all_to_all(slot_grads, 'vocab', split_axis=1, concat_axis=0, tiled=True)]
    all_gather x2 -> x0, waiting for transfers between devices: 82 us -> none  [the longest x1 72.4 us: local(): lax.all_gather(master_new.astype(jnp.bfloat16), 'dp', axis=0, tiled=True)]
    unnamed x1 -> x0, blocking collectives: 77.9 us -> none
    all_to_all x2 -> x0, starting transfers between devices: 19.6 us -> none  [the longest x1 15.5 us: local(): lax.all_to_all(slot_ids, 'vocab', split_axis=1, concat_axis=0, tiled=True)]
    unnamed x4 -> x0, starting transfers between devices: 13.5 us -> none
    unnamed x22 -> x10, local copies, waits for them, and re-layouts: 17.1 us -> 3.7 us
    dot_general x2 -> x0, matrix products: 10.2 us -> none  [the longest x1 7.56 us: local(): lax.dot_general(masked, lax.all_gather(hidden, 'vocab', axis=1, tiled=Tru...]
  transfers between devices with their start and end apart: 8 -> 0, of which waited for: 7 -> 0; matrix products, arithmetic and copies ran while one was open for 2% -> 0% of each run, Pallas kernels for 0% -> 0%
where the time goes in v1:
time: 181 us
  Pallas kernels  171 us (94%)
  local copies, waits for them, and re-layouts  7.62 us (4%)
  other arithmetic  2.09 us (1%)
    pallas_call x1, Pallas kernels, local(): pl.pallas_call(kernel, out_shape=(jax.ShapeDtypeStruct((12, 5120), F32),...  171 us
    transpose x1, local copies, waits for them, and re-layouts, local(): table = out[3].transpose(0, 1, 3, 2, 4).reshape(192, 5120)  3.76 us
    unnamed x10, local copies, waits for them, and re-layouts  3.7 us

profile of v1, /device:TPU:6, one launch (start us, length us, event | category | flops | bytes accessed | tf_op | source)
XLA Modules:
  0.0 181.1 jit_solution(17178964431494738794)
XLA Ops:
  0.7 0.7 broadcast_add_fusion
  1.4 0.7 fusion.7
  2.1 0.1 copy.14
  2.2 0.7 compare_select_fusion.ids
  2.9 170.7 %shard_map.120 = (f32[12,5120]{1,0:T(8,128)}, f32[12,5120]{1,0:T(8,128)}, f32[12,5120]{1,0:T(8,128)}, bf16[4,4,2,12,2560]{4,3,2,1,0:T(8,128)(2,1)}) custom-call(bf16[160,1024]{1,0:T(8,128)(2,1)} %bitcast.24, bf16[192,1024]{1,0:T(8,128)(2,1)} %bitcast.23, s32[1,1024]{1,0:T(1,128)} %bitcast.25, bf16[192,5120]{1,0:T(8,128)(2,1)} %bitcast.21, ...), custom_call_target="tpu_custom_call" | custom-call | tf_op jit(solution)/shard_map/pallas_call | solution.py:421
  173.6 3.8 %copy.15 = bf16[4,4,12,2,2560]{4,3,2,1,0:T(2,128)(2,1)S(1)} copy(bf16[4,4,12,2,2560]{4,2,3,1,0:T(8,128)(2,1)} %bitcast.20) | data formatting | bytes 3932160 | tf_op jit(solution)/shard_map/transpose | solution.py:454
  177.4 0.0 copy-start.2
  177.4 0.0 copy-start.1
  177.4 0.0 copy-start
  177.4 1.5 copy.17
  178.9 0.0 copy-done.2
  178.9 0.7 copy.22
  179.7 0.0 copy-done.1
  179.7 0.7 copy.23
  180.4 0.0 copy-done
  180.4 0.7 copy.24
  (5 shorter events, 0.1 us)
Async XLA Ops:
  177.4 1.5 copy-start.2
  177.4 2.3 %copy-start.1 = (f32[12,5120]{1,0:T(8,128)S(1)}, f32[12,5120]{1,0:T(8,128)}, u32[]{:S(2)}) copy-start(f32[12,5120]{1,0:T(8,128)} %get-tuple-element.17) | copy-start | bytes 737284
  177.4 3.0 %copy-start = (f32[12,5120]{1,0:T(8,128)S(1)}, f32[12,5120]{1,0:T(8,128)}, u32[]{:S(2)}) copy-start(f32[12,5120]{1,0:T(8,128)} %get-tuple-element.18) | copy-start | bytes 737284

commit v2 on v1

v2 whole, which is shorter than its diff:
```python
import jax
import jax.numpy as jnp
from jax import lax
from jax.experimental import pallas as pl
from jax.experimental.pallas import tpu as pltpu
from jax.sharding import PartitionSpec as P

STEP = 8
Z = 16
NX = 4
NY = 4
DP = NX * NY
COLS = 640
NB = 8
UNITS = 48
PARTS = 4
PU = UNITS // PARTS
HALF = ((0, 384), (384, 256))
MESH = pl.DeviceIdType.MESH
F32 = jnp.float32
BF16 = jnp.bfloat16


def update(g, m, mu, nu):
    fn = 0.9 * mu + 0.1 * g
    sn = 0.95 * nu + 0.05 * g * g
    corr1 = 1.0 / (1.0 - 0.9**STEP)
    corr2 = 1.0 / (1.0 - 0.95**STEP)
    mn = m - 0.05 * (fn * corr1 / (jnp.sqrt(sn * corr2) + 1e-08) + 0.1 * m)
    return mn, fn, sn


def kernel(
    hid, logit, mask, slots, rows_in, counts, master, first, second,
    grad_o, table,
    hall, masked, outbox, inbox, part0, part1, ring0, ring1, head, ra, r1, q, r2, grad, emb0, emb1, tags_v, ta, tb,
    ag_s, ag_r, sib_s, sib_r, sl_s, sl_r, z_s, z_r,
    ra_s, ra_r, r1_s, r1_r, r2_s, r2_r, e_s, e_r, t1_s, t1_r, t2_s, t2_r, t3_s, t3_r, loc,
):
    d = lax.axis_index("dp")
    v = lax.axis_index("vocab")
    z, c = v // 2, v % 2
    y, x = d // NX, d % NX
    pg, h = d // 2, d % 2
    me = d * 2 + c

    def rc(src, dst, ss, rs, dev):
        return pltpu.make_async_remote_copy(
            src_ref=src, dst_ref=dst, send_sem=ss, recv_sem=rs,
            device_id=dev, device_id_type=MESH)

    up = (d, (v + 2) % 32)
    down = (d, (v + 30) % 32)
    sib = (d, z * 2 + (1 - c))
    zdir = (d, (v + 2 + 28 * c) % 32)

    bar = pltpu.get_barrier_semaphore()
    pl.semaphore_signal(bar, inc=1, device_id=up, device_id_type=MESH)
    pl.semaphore_signal(bar, inc=1, device_id=down, device_id_type=MESH)

    def greet(k, carry):
        o = (me + k) % 32
        pl.semaphore_signal(bar, inc=1, device_id=(o // 2, z * 2 + o % 2), device_id_type=MESH)
        return carry

    lax.fori_loop(1, 32, greet, 0)
    pl.semaphore_wait(bar, 33)

    def plane_at(sg, s):
        return (z - s + 16) % 16 if sg == 0 else (z + s) % 16

    def ag(sg, s, half):
        idx = plane_at(sg, s - 1) * 2 + c
        rows = pl.ds(80 * half, 80)
        ref = hall.at[idx, rows]
        src = hid.at[rows] if s == 1 else ref
        return rc(src, ref, ag_s.at[sg, s, half], ag_r.at[sg, s, half], up if sg == 0 else down)

    def ag_arrival(sg, s, half):
        idx = plane_at(sg, s) * 2 + c
        ref = hall.at[idx, pl.ds(80 * half, 80)]
        rc(ref, ref, ag_s.at[sg, s, half], ag_r.at[sg, s, half], up).wait_recv()

    def share(sg, s, half):
        idx = plane_at(sg, s) * 2 + c
        ref = hall.at[idx, pl.ds(80 * half, 80)]
        return rc(ref, ref, sib_s.at[sg, s, half], sib_r.at[sg, s, half], sib)

    def share_arrival(sg, s, half):
        idx = plane_at(sg, s) * 2 + 1 - c
        ref = hall.at[idx, pl.ds(80 * half, 80)]
        rc(ref, ref, sib_s.at[sg, s, half], sib_r.at[sg, s, half], sib).wait_recv()

    own_share = rc(hid, hall.at[v], sib_s.at[0, 0, 0], sib_r.at[0, 0, 0], sib)
    for half in (0, 1):
        ag(0, 1, half).start()
        ag(1, 1, half).start()
    own_share.start()
    own_copy = pltpu.make_async_copy(hid, hall.at[v], loc.at[0])
    own_copy.start()

    part, ring, emb, rowsets = (part0, part1), (ring0, ring1), (emb0, emb1), (ta, tb)

    def row_maps(width):
        r = lax.broadcasted_iota(jnp.int32, (256, width), 0)
        k = lax.broadcasted_iota(jnp.int32, (256, width), 1)
        i = (r // 8) % 8
        to_plane = jnp.where((r // 64) % 2 == 0, z + 24 - i, z + 9 + i) % 16
        return k, r % 8, i, to_plane * 2 + r // 128

    k, e, _, owner = row_maps(192)
    select = jnp.where((e < 6) & (e * 32 + owner == k), 1.0, 0.0).astype(BF16)
    k, e, _, owner = row_maps(32)
    pick = jnp.where((e == 6) & (owner == k), 1.0, 0.0).astype(BF16)
    live = lax.broadcasted_iota(jnp.int32, (6, 32), 0) < counts[...]
    tag = jnp.where(live, rows_in[:, 0, :] + 1, 0).astype(F32)
    tag = jnp.concatenate([tag, jnp.zeros((2, 32), F32)], axis=0).astype(BF16)
    tag = lax.dot_general(pick, tag, (((1,), (1,)), ((), ())), preferred_element_type=F32)
    a = lax.broadcasted_iota(jnp.int32, (8, COLS), 0)
    b = lax.broadcasted_iota(jnp.int32, (8, COLS), 1)
    spread = jnp.where((b % 8 == a) & (b // 16 == me), 1.0, 0.0).astype(BF16)
    tag = jnp.dot(tag.astype(BF16), spread, preferred_element_type=F32)
    k, _, i, _ = row_maps(COLS)
    tags_v[...] = jnp.where((k // 8) % 2 == i % 2, tag, 0.0)

    def slot_copy(g, w):
        to = (2 * g + w // 2, z * 2 + w % 2)
        return rc(outbox.at[g, w], inbox.at[me], sl_s.at[g * 4 + w], sl_r.at[me], to)

    def send_slots(g, carry):
        cols = pl.ds(pl.multiple_of(g * COLS, 128), COLS)
        rows = jnp.dot(select, slots[:, cols], preferred_element_type=F32) + tags_v[...]
        outbox[g] = rows.astype(BF16).reshape(4, 64, COLS)
        for w in range(4):
            mine = (2 * g + w // 2 == d) & (w % 2 == c)

            @pl.when(mine)
            def _():
                pltpu.make_async_copy(outbox.at[g, w], inbox.at[me], sl_r.at[me]).start()

            @pl.when(jnp.logical_not(mine))
            def _():
                slot_copy(g, w).start()
        return carry

    lax.fori_loop(0, 2, send_slots, 0)
    kz = z // 2

    def block_of(n):
        t = (n + 1) // 2
        return (kz + 16 + jnp.where(n % 2 == 1, -t, t)) % NB

    def at_axis(g, xfirst):
        return (y * NX + g, v) if xfirst else (g * NX + x, v)

    def stage0(n, side, xfirst):
        mine = x if xfirst else y
        opp, to = (mine + 2) % 4, (mine + 1 + 2 * side) % 4
        rows = pl.ds(2 * side, 2)
        ref = head.at[n, rows, opp] if xfirst else head.at[n, opp, rows]
        return rc(ref, ra.at[n, side], ra_s.at[n, side], ra_r.at[n, side], at_axis(to, xfirst))

    def stage1(n, side, xfirst):
        to = ((x if xfirst else y) + 1 + 2 * side) % 4
        ref = head.at[n, :, to] if xfirst else head.at[n, to]
        return rc(ref, r1.at[n, side], r1_s.at[n, side], r1_r.at[n, side], at_axis(to, xfirst))

    def stage2(n, g, xfirst):
        if xfirst:
            return rc(q.at[n, g], r2.at[n, y], r2_s.at[n, g], r2_r.at[n, y], (g * NX + x, v))
        return rc(q.at[n, g], r2.at[n, x], r2_s.at[n, g], r2_r.at[n, x], (y * NX + g, v))

    def head_block(n):
        kb = block_of(n)
        rows = hall[pl.ds(4 * kb, 4)].reshape(COLS, 1024)
        val = lax.dot_general(masked[...], rows, (((1,), (1,)), ((), ())), preferred_element_type=F32)
        head[n] = val.reshape(NY, NX, 3, 4, COLS)

    def head_send(n):
        for side in (0, 1):
            stage0(n, side, n % 2 == 0).start()

    def head_add(n):
        xfirst = n % 2 == 0
        mine = x if xfirst else y
        for side in (0, 1):
            ref = ra.at[n, side]
            rc(ref, ref, ra_s.at[n, side], ra_r.at[n, side], up).wait_recv()
            to = (mine + 1 + 2 * side) % 4
            rows = pl.ds(2 * side, 2)
            if xfirst:
                head[n, rows, to] = head[n, rows, to] + ra[n, side]
            else:
                head[n, to, rows] = head[n, to, rows] + ra[n, side]
            stage1(n, side, xfirst).start()

    def head_mid(n):
        xfirst = n % 2 == 0
        for side in (0, 1):
            ref = r1.at[n, side]
            rc(ref, ref, r1_s.at[n, side], r1_r.at[n, side], up).wait_recv()
        own = head[n, :, x] if xfirst else head[n, y]
        q[n] = own + r1[n, 0] + r1[n, 1]
        then = y if xfirst else x
        for o in range(1, 4):
            stage2(n, (then + o) % 4, xfirst).start()

    def head_end(n):
        xfirst = n % 2 == 0
        then = y if xfirst else x
        for o in range(1, 4):
            src = (then + o) % 4
            ref = r2.at[n, src]
            rc(ref, ref, r2_s.at[n, src], r2_r.at[n, src], up).wait_recv()
        grad[block_of(n)] = (
            q[n, then] + r2[n, (then + 1) % 4] + r2[n, (then + 2) % 4] + r2[n, (then + 3) % 4]
        )

    def ag_step(s):
        for half in (0, 1):
            for sg in (0, 1):
                if s == 8 and half != sg:
                    continue
                ag_arrival(sg, s, half)
                if s < 7 or (s == 7 and half == sg):
                    ag(sg, s + 1, half).start()
                share(sg, s, half).start()

    def shares_of(s):
        for half in (0, 1):
            for sg in (0, 1):
                if s == 8 and half != sg:
                    continue
                share_arrival(sg, s, half)

    def embed_parts():
        def arrived(s, carry):
            rc(inbox.at[s], inbox.at[s], sl_s.at[s], sl_r.at[s], up).wait_recv()
            return carry

        lax.fori_loop(0, 32, arrived, 0)

        def pair(p, carry):
            rows = inbox[:, pl.ds(pl.multiple_of(16 * p, 16), 16), :]
            tags = rows[:, :, :512].astype(F32)
            sub = lax.broadcasted_iota(jnp.int32, (32, 16, 512), 1)
            tags = jnp.where(sub % 8 == 6, tags, 0.0)
            tags = jnp.sum(jnp.sum(tags, axis=0), axis=0, keepdims=True)
            lane = lax.broadcasted_iota(jnp.int32, (1, 512), 1)
            shift = jnp.where((lane // 8) % 2 == 1, 192.0, 0.0)
            tags = jnp.where(tags > 0.5, tags + shift, 0.0)
            row = lax.broadcasted_iota(jnp.int32, (384, 512), 0).astype(F32) + 1.0
            hot = jnp.where(row == tags, 1.0, 0.0).astype(BF16)
            val = jnp.dot(hot, rows.reshape(512, COLS), preferred_element_type=F32)
            for a, (off, n) in enumerate(HALF):
                part[a][pl.ds(2 * p, 2)] = val[:, off:off + n].reshape(2, UNITS, 4, n)
            return carry

        lax.fori_loop(0, 4, pair, 0)

    def z_copy(s, src, p, a):
        rows = pl.ds(p * PU, PU)
        return rc(src.at[rows], ring[a].at[s, rows], z_s.at[a, s, p], z_r.at[a, s, p], zdir)

    def z_arrival(s, p, a):
        ref = ring[a].at[s, pl.ds(p * PU, PU)]
        rc(ref, ref, z_s.at[a, s, p], z_r.at[a, s, p], zdir).wait_recv()

    def z_step(s, a):
        for p in range(PARTS):
            if s == 0:
                z_copy(0, part[a].at[0], p, a).start()
                continue
            z_arrival(s - 1, p, a)
            rows = pl.ds(p * PU, PU)
            ring[a][s - 1, rows] = ring[a][s - 1, rows] + part[a][s, rows]
            if s < 7:
                z_copy(s, ring[a].at[s - 1], p, a).start()
            else:

                @pl.when(c == 0)
                def _():
                    z_copy(s, ring[a].at[s - 1], p, a).start()

    fin = 7 - c

    def e_refs(t, a):
        return ring[a].at[fin, pl.ds(3 * t, 3)], emb[a].at[c, pg]

    def e_copy(t, a):
        src, dst = e_refs(t, a)
        return rc(src, dst, e_s.at[a, t], e_r.at[a, c, pg], (t, z * 2 + h))

    def finish(a):
        for p in range(PARTS):

            @pl.when(c == 0)
            def _():
                z_arrival(7, p, a)

            for t in range(4 * p, 4 * p + 4):
                mine = (t == d) & (h == c)

                @pl.when(mine)
                def _():
                    src, dst = e_refs(t, a)
                    pltpu.make_async_copy(src, dst, e_r.at[a, c, pg]).start()

                @pl.when(jnp.logical_not(mine))
                def _():
                    e_copy(t, a).start()

    def adam(a):
        off, n = HALF[a]
        for b in range(NB):
            cut = pl.ds(off, n)
            for w in (0, 1):
                ref = emb[a].at[w, b]
                rc(ref, ref, e_s.at[a, b], e_r.at[a, w, b], up).wait_recv()
            g = grad[b, :, :, cut] + emb[a][0, b] + emb[a][1, b]
            g = jnp.concatenate([g[0], g[1], g[2]], axis=0)
            cols = pl.ds(b * COLS + off, n)
            mn, _, _ = update(g, master[:, cols], first[:, cols], second[:, cols])
            grad_o[:, cols] = g
            mn = mn.astype(BF16)
            for u in range(3):
                rowsets[a][b // 4, y, x, u, :, pl.ds((b % 4) * n, n)] = mn[4 * u:4 * u + 4]

    firsts = (x, y)
    seconds = (y, x)

    def group(a, w, g):
        return rowsets[a].at[w, g] if w == 0 else rowsets[a].at[w, :, g]

    def t1(a, w, g):
        ref = rowsets[a].at[w, y, x]
        to = (y * NX + g, v) if w == 0 else (g * NX + x, v)
        return rc(ref, ref, t1_s.at[a, w, g], t1_r.at[a, w, firsts[w]], to)

    def t2(a, w, side):
        ref = group(a, w, seconds[w])
        to = at_axis((seconds[w] + 1 + 2 * side) % 4, w == 1)
        return rc(ref, ref, t2_s.at[a, w, side], t2_r.at[a, w, side], to)

    def t3(a, w, side):
        g = (seconds[w] + 3 + 2 * side) % 4
        ref = group(a, w, g).at[pl.ds(2 * side, 2)]
        to = at_axis((seconds[w] + 1 + 2 * side) % 4, w == 1)
        return rc(ref, ref, t3_s.at[a, w, side], t3_r.at[a, w, side], to)

    def spread_rows(a):
        for o in range(1, 4):
            for w in (0, 1):
                t1(a, w, (firsts[w] + o) % 4).start()

    def spread_groups(a):
        for w in (0, 1):
            for o in range(1, 4):
                g = (firsts[w] + o) % 4
                ref = rowsets[a].at[w, y, g] if w == 0 else rowsets[a].at[w, g, x]
                rc(ref, ref, t1_s.at[a, w, g], t1_r.at[a, w, g], up).wait_recv()
            for side in (0, 1):
                t2(a, w, side).start()

    def pass_groups(a):
        for w in (0, 1):
            for side in (0, 1):
                ref = group(a, w, (seconds[w] + 3 + 2 * side) % 4)
                rc(ref, ref, t2_s.at[a, w, side], t2_r.at[a, w, side], up).wait_recv()
                t3(a, w, side).start()

    def gathered(a):
        for w in (0, 1):
            for side in (0, 1):
                ref = group(a, w, (seconds[w] + 2) % 4).at[pl.ds(2 * side, 2)]
                rc(ref, ref, t3_s.at[a, w, side], t3_r.at[a, w, side], up).wait_recv()

    def write_table(a):
        off, n = HALF[a]
        for w in (0, 1):
            for b in range(4):
                for m in range(12):
                    units = [4 * m + i for i in range(4)]
                    cut = pl.ds(b * n, n)
                    rows = [rowsets[a][w, t // 12, (t // 3) % 4, t % 3, :, cut] for t in units]
                    table[pl.ds(16 * m, 16), pl.ds((4 * w + b) * COLS + off, n)] = jnp.concatenate(rows, axis=0)

    own_copy.wait()
    ag_step(1)
    lax.fori_loop(2, 5, send_slots, 0)
    ag_step(2)
    lax.fori_loop(5, 8, send_slots, 0)
    own_idx = v + 1 - 2 * c
    rc(hid, hall.at[own_idx], sib_s.at[0, 0, 0], sib_r.at[0, 0, 0], sib).wait_recv()
    masked[...] = logit[...] * mask[...].astype(BF16)
    ag_step(3)
    shares_of(1)
    head_block(0)
    shares_of(2)
    shares_of(3)
    ag_step(4)
    head_block(1)
    head_block(2)
    ag_step(5)
    shares_of(4)
    shares_of(5)
    head_block(3)
    ag_step(6)
    head_block(4)
    ag_step(7)
    embed_parts()
    z_step(0, 0)
    for n in range(5):
        head_send(n)
    shares_of(6)
    shares_of(7)
    head_block(5)
    head_block(6)
    head_send(5)
    head_send(6)
    ag_step(8)
    z_step(1, 0)
    shares_of(8)
    head_block(7)
    head_send(7)
    head_add(0)
    head_add(1)
    z_step(2, 0)
    head_add(2)
    head_add(3)
    z_step(3, 0)
    head_mid(0)
    head_mid(1)
    head_add(4)
    z_step(4, 0)
    head_mid(2)
    head_mid(3)
    head_add(5)
    z_step(5, 0)
    head_mid(4)
    head_end(0)
    head_end(1)
    head_add(6)
    z_step(6, 0)
    z_step(0, 1)
    head_mid(5)
    head_end(2)
    head_end(3)
    head_add(7)
    z_step(7, 0)
    z_step(1, 1)
    finish(0)
    head_mid(6)
    head_end(4)
    z_step(2, 1)
    head_mid(7)
    head_end(5)
    z_step(3, 1)
    head_end(6)
    head_end(7)
    z_step(4, 1)
    adam(0)
    spread_rows(0)
    z_step(5, 1)
    z_step(6, 1)
    spread_groups(0)
    z_step(7, 1)
    finish(1)
    pass_groups(0)
    gathered(0)
    write_table(0)
    adam(1)
    spread_rows(1)
    spread_groups(1)
    pass_groups(1)
    gathered(1)
    write_table(1)

    own_share.wait_send()
    for s in range(1, 9):
        for half in (0, 1):
            for sg in (0, 1):
                if s == 8 and half != sg:
                    continue
                ag(sg, s, half).wait_send()
                share(sg, s, half).wait_send()

    def slots_left(g, carry):
        for w in range(4):

            @pl.when(jnp.logical_not((2 * g + w // 2 == d) & (w % 2 == c)))
            def _():
                slot_copy(g, w).wait_send()
        return carry

    lax.fori_loop(0, NB, slots_left, 0)
    for n in range(NB):
        xfirst = n % 2 == 0
        for side in (0, 1):
            stage0(n, side, xfirst).wait_send()
            stage1(n, side, xfirst).wait_send()
        for o in range(1, 4):
            stage2(n, ((y if xfirst else x) + o) % 4, xfirst).wait_send()
    for a in (0, 1):
        for s in range(8):
            for p in range(PARTS):
                src = part[a].at[0] if s == 0 else ring[a].at[s - 1]
                if s < 7:
                    z_copy(s, src, p, a).wait_send()
                else:

                    @pl.when(c == 0)
                    def _():
                        z_copy(s, src, p, a).wait_send()
        for t in range(DP):

            @pl.when(jnp.logical_not((t == d) & (h == c)))
            def _():
                e_copy(t, a).wait_send()
        for w in (0, 1):
            for o in range(1, 4):
                t1(a, w, (firsts[w] + o) % 4).wait_send()
            for side in (0, 1):
                t2(a, w, side).wait_send()
                t3(a, w, side).wait_send()


def local(hidden, logit_grad, predict_mask, slot_grads, slot_rows, slot_counts, master, first, second):
    slots = slot_grads[0].transpose(1, 0, 2).reshape(192, 5120)
    rows_in = slot_rows.transpose(2, 0, 1)
    vm = pl.BlockSpec(memory_space=pltpu.VMEM)
    dma = pltpu.SemaphoreType.DMA
    grad, table = pl.pallas_call(
        kernel,
        out_shape=(
            jax.ShapeDtypeStruct((12, 5120), F32),
            jax.ShapeDtypeStruct((192, 5120), BF16),
        ),
        in_specs=[vm] * 9,
        out_specs=(vm,) * 2,
        scratch_shapes=[
            pltpu.VMEM((32, 160, 1024), BF16),
            pltpu.VMEM((192, 1024), BF16),
            pltpu.VMEM((NB, 4, 64, COLS), BF16),
            pltpu.VMEM((32, 64, COLS), BF16),
            pltpu.VMEM((8, UNITS, 4, HALF[0][1]), F32),
            pltpu.VMEM((8, UNITS, 4, HALF[1][1]), F32),
            pltpu.VMEM((8, UNITS, 4, HALF[0][1]), F32),
            pltpu.VMEM((8, UNITS, 4, HALF[1][1]), F32),
            pltpu.VMEM((NB, NY, NX, 3, 4, COLS), F32),
            pltpu.VMEM((NB, 2, 2, 3, 4, COLS), F32),
            pltpu.VMEM((NB, 2, 4, 3, 4, COLS), F32),
            pltpu.VMEM((NB, 4, 3, 4, COLS), F32),
            pltpu.VMEM((NB, 4, 3, 4, COLS), F32),
            pltpu.VMEM((NB, 3, 4, COLS), F32),
            pltpu.VMEM((2, NB, 3, 4, HALF[0][1]), F32),
            pltpu.VMEM((2, NB, 3, 4, HALF[1][1]), F32),
            pltpu.VMEM((256, COLS), F32),
            pltpu.VMEM((2, NY, NX, 3, 4, 4 * HALF[0][1]), BF16),
            pltpu.VMEM((2, NY, NX, 3, 4, 4 * HALF[1][1]), BF16),
            dma((2, 9, 2)), dma((2, 9, 2)), dma((2, 9, 2)), dma((2, 9, 2)),
            dma((32,)), dma((32,)), dma((2, 8, PARTS)), dma((2, 8, PARTS)),
            dma((NB, 2)), dma((NB, 2)), dma((NB, 2)), dma((NB, 2)), dma((NB, 4)), dma((NB, 4)),
            dma((2, DP)), dma((2, 2, NB)),
            dma((2, 2, 4)), dma((2, 2, 4)), dma((2, 2, 2)), dma((2, 2, 2)), dma((2, 2, 2)), dma((2, 2, 2)),
            dma((1,)),
        ],
        compiler_params=pltpu.CompilerParams(
            collective_id=0, has_side_effects=True, vmem_limit_bytes=60 * 1024 * 1024),
    )(hidden.T, logit_grad.T, predict_mask[None, :], slots, rows_in, slot_counts, master, first, second)
    return (*update(grad, master, first, second), table)


def solution(mesh):
    in_specs = (
        P("dp", "vocab"),
        P("dp", "vocab"),
        P("dp"),
        P(("dp", "vocab"), None, None, None),
        P(("dp", "vocab"), None, None),
        P(("dp", "vocab"), None),
        P(("vocab", "dp"), None),
        P(("vocab", "dp"), None),
        P(("vocab", "dp"), None),
    )
    out_specs = (
        P(("vocab", "dp"), None),
        P(("vocab", "dp"), None),
        P(("vocab", "dp"), None),
        P("vocab", None),
    )
    return jax.shard_map(local, mesh=mesh, in_specs=in_specs, out_specs=out_specs, check_vma=False)
```

time: 181 us -> 157 us (0.87)
  Pallas kernels: 171 us -> 151 us
  local copies, waits for them, and re-layouts: 7.62 us -> 1.29 us
    pallas_call x1, Pallas kernels: 171 us -> 151 us  [local(): pl.pallas_call(kernel, out_shape=(jax.ShapeDtypeStruct((12, 5120), F32),...]
    transpose x1 -> x0, local copies, waits for them, and re-layouts: 3.76 us -> none  [local(): table = out[3].transpose(0, 1, 3, 2, 4).reshape(192, 5120)]
    unnamed x10 -> x9, local copies, waits for them, and re-layouts: 3.7 us -> 1.29 us
    sub x0 -> x1, other arithmetic: none -> 2.2 us  [update(): mn = m - 0.05 * (fn * corr1 / (jnp.sqrt(sn * corr2) + 1e-08) + 0.1 * m)]
where the time goes in v2:
time: 157 us; the launch traced here: 155 us
  Pallas kernels  151 us (96%)
  other arithmetic  2.2 us (1%)
    pallas_call x1, Pallas kernels, local(): pl.pallas_call(kernel, out_shape=(jax.ShapeDtypeStruct((12, 5120), F32),...  151 us

profile of v2, /device:TPU:6, one launch (start us, length us, event | category | flops | bytes accessed | tf_op | source)
XLA Modules:
  0.0 155.4 jit_solution(1124990478908263153)
XLA Ops:
  0.6 0.0 copy-start.3
  0.6 0.0 copy-start.2
  0.7 0.0 copy-start.1
  0.7 151.2 %shard_map.120 = (f32[12,5120]{1,0:T(8,128)}, bf16[192,5120]{1,0:T(8,128)(2,1)}) custom-call(bf16[160,1024]{1,0:T(8,128)(2,1)} %bitcast.11, bf16[192,1024]{1,0:T(8,128)(2,1)} %bitcast.10, s32[1,1024]{1,0:T(1,128)} %bitcast.12, bf16[192,5120]{1,0:T(8,128)(2,1)} %bitcast.9, s32[6,1,32]{2,1,0:T(1,128)} %bitcast.13, s32[1,32]{1,0:T(1,128)} %counts.1, ...), custom_call_target="tpu_custom_call" | custom-call | tf_op jit(solution)/shard_map/pallas_call | solution.py:533
  151.9 0.0 copy-start
  151.9 0.0 copy-done.3
  151.9 0.0 copy-done.2
  151.9 0.0 copy-done.1
  151.9 2.2 %multiply_subtract_fusion = (f32[12,5120]{1,0:T(8,128)}, f32[12,5120]{1,0:T(8,128)}, f32[12,5120]{1,0:T(8,128)}) fusion(f32[12,5120]{1,0:T(8,128)S(1)} %copy-done.1, f32[12,5120]{1,0:T(8,128)} %get-tuple-element.6, f32[12,5120]{1,0:T(8,128)S(1)} %copy-done.2, f32[12,5120]{1,0:T(8,128)S(1)} %copy-done.3), kind=kLoop, calls=%fused_computation.2 | loop fusion | flops 921600 | bytes 1720320 | tf_op jit(solution)/shard_map/sub | solution.py:29
  154.1 0.0 copy-done
  154.1 1.3 copy.14
Async XLA Ops:
  0.6 151.2 %copy-start.3 = (f32[12,5120]{1,0:T(8,128)S(1)}, f32[12,5120]{1,0:T(8,128)}, u32[]{:S(2)}) copy-start(f32[12,5120]{1,0:T(8,128)} %second.1) | copy-start | bytes 737284
  0.6 151.2 %copy-start.2 = (f32[12,5120]{1,0:T(8,128)S(1)}, f32[12,5120]{1,0:T(8,128)}, u32[]{:S(2)}) copy-start(f32[12,5120]{1,0:T(8,128)} %first.1) | copy-start | bytes 737284
  0.7 151.2 %copy-start.1 = (f32[12,5120]{1,0:T(8,128)S(1)}, f32[12,5120]{1,0:T(8,128)}, u32[]{:S(2)}) copy-start(f32[12,5120]{1,0:T(8,128)} %master.1) | copy-start | bytes 737284
  151.9 2.2 %copy-start = (bf16[192,5120]{1,0:T(8,128)(2,1)S(1)}, bf16[192,5120]{1,0:T(8,128)(2,1)}, u32[]{:S(2)}) copy-start(bf16[192,5120]{1,0:T(8,128)(2,1)} %get-tuple-element.18) | copy-start | bytes 5898244

commit v3 on v2

--- a/solution.py
+++ b/solution.py
@@ -31,9 +31,9 @@
 
 
 def kernel(
-    hid, logit, mask, slots, rows_in, counts, master, first, second,
+    hid, logit, mask, slots_in, rows_in, counts, master_in, first_in, second_in,
     grad_o, table,
-    hall, masked, outbox, inbox, part0, part1, ring0, ring1, head, ra, r1, q, r2, grad, emb0, emb1, tags_v, ta, tb,
+    slots, master, first, second, hall, masked, outbox, inbox, part0, part1, ring0, ring1, head, ra, r1, q, r2, grad, emb0, emb1, tags_v, ta, tb,
     ag_s, ag_r, sib_s, sib_r, sl_s, sl_r, z_s, z_r,
     ra_s, ra_r, r1_s, r1_r, r2_s, r2_r, e_s, e_r, t1_s, t1_r, t2_s, t2_r, t3_s, t3_r, loc,
 ):
@@ -53,6 +53,14 @@
     down = (d, (v + 30) % 32)
     sib = (d, z * 2 + (1 - c))
     zdir = (d, (v + 2 + 28 * c) % 32)
+
+    fetches = [
+        pltpu.make_async_copy(src, dst, loc.at[i + 1])
+        for i, (src, dst) in enumerate((
+            (slots_in, slots), (logit, masked), (master_in, master), (first_in, first), (second_in, second)))
+    ]
+    for fetch in fetches:
+        fetch.start()
 
     bar = pltpu.get_barrier_semaphore()
     pl.semaphore_signal(bar, inc=1, device_id=up, device_id_type=MESH)
@@ -123,27 +131,40 @@
     k, _, i, _ = row_maps(COLS)
     tags_v[...] = jnp.where((k // 8) % 2 == i % 2, tag, 0.0)
 
-    def slot_copy(g, w):
+    def slot_copy(g, w, part_of):
+        rows = pl.ds(32 * part_of, 32)
         to = (2 * g + w // 2, z * 2 + w % 2)
-        return rc(outbox.at[g, w], inbox.at[me], sl_s.at[g * 4 + w], sl_r.at[me], to)
+        return rc(outbox.at[g, w, rows], inbox.at[me, rows],
+                  sl_s.at[part_of, g * 4 + w], sl_r.at[part_of, me], to)
+
+    def post(g, part_of):
+        rows = pl.ds(32 * part_of, 32)
+        for w in range(4):
+            mine = (2 * g + w // 2 == d) & (w % 2 == c)
+
+            @pl.when(mine)
+            def _():
+                pltpu.make_async_copy(
+                    outbox.at[g, w, rows], inbox.at[me, rows], sl_r.at[part_of, me]).start()
+
+            @pl.when(jnp.logical_not(mine))
+            def _():
+                slot_copy(g, w, part_of).start()
 
     def send_slots(g, carry):
         cols = pl.ds(pl.multiple_of(g * COLS, 128), COLS)
         rows = jnp.dot(select, slots[:, cols], preferred_element_type=F32) + tags_v[...]
         outbox[g] = rows.astype(BF16).reshape(4, 64, COLS)
-        for w in range(4):
-            mine = (2 * g + w // 2 == d) & (w % 2 == c)
-
-            @pl.when(mine)
-            def _():
-                pltpu.make_async_copy(outbox.at[g, w], inbox.at[me], sl_r.at[me]).start()
-
-            @pl.when(jnp.logical_not(mine))
-            def _():
-                slot_copy(g, w).start()
+        post(g, 0)
         return carry
 
+    def send_rest(g, carry):
+        post(g, 1)
+        return carry
+
+    fetches[0].wait()
     lax.fori_loop(0, 2, send_slots, 0)
+
     kz = z // 2
 
     def block_of(n):
@@ -233,9 +254,10 @@
                     continue
                 share_arrival(sg, s, half)
 
-    def embed_parts():
+    def embed_parts(part_of):
         def arrived(s, carry):
-            rc(inbox.at[s], inbox.at[s], sl_s.at[s], sl_r.at[s], up).wait_recv()
+            ref = inbox.at[s, pl.ds(32 * part_of, 32)]
+            rc(ref, ref, sl_s.at[part_of, s], sl_r.at[part_of, s], up).wait_recv()
             return carry
 
         lax.fori_loop(0, 32, arrived, 0)
@@ -256,7 +278,7 @@
                 part[a][pl.ds(2 * p, 2)] = val[:, off:off + n].reshape(2, UNITS, 4, n)
             return carry
 
-        lax.fori_loop(0, 4, pair, 0)
+        lax.fori_loop(2 * part_of, 2 * part_of + 2, pair, 0)
 
     def z_copy(s, src, p, a):
         rows = pl.ds(p * PU, PU)
@@ -311,6 +333,9 @@
                     e_copy(t, a).start()
 
     def adam(a):
+        if a == 0:
+            for fetch in fetches[2:]:
+                fetch.wait()
         off, n = HALF[a]
         for b in range(NB):
             cut = pl.ds(off, n)
@@ -392,8 +417,10 @@
     lax.fori_loop(5, 8, send_slots, 0)
     own_idx = v + 1 - 2 * c
     rc(hid, hall.at[own_idx], sib_s.at[0, 0, 0], sib_r.at[0, 0, 0], sib).wait_recv()
-    masked[...] = logit[...] * mask[...].astype(BF16)
+    fetches[1].wait()
+    masked[...] = masked[...] * mask[...].astype(BF16)
     ag_step(3)
+    lax.fori_loop(0, 8, send_rest, 0)
     shares_of(1)
     head_block(0)
     shares_of(2)
@@ -408,7 +435,7 @@
     ag_step(6)
     head_block(4)
     ag_step(7)
-    embed_parts()
+    embed_parts(0)
     z_step(0, 0)
     for n in range(5):
         head_send(n)
@@ -428,32 +455,33 @@
     z_step(2, 0)
     head_add(2)
     head_add(3)
+    head_add(4)
     z_step(3, 0)
+    embed_parts(1)
+    z_step(4, 0)
     head_mid(0)
     head_mid(1)
-    head_add(4)
-    z_step(4, 0)
+    head_add(5)
+    head_add(6)
+    head_add(7)
+    z_step(5, 0)
     head_mid(2)
     head_mid(3)
-    head_add(5)
-    z_step(5, 0)
     head_mid(4)
-    head_end(0)
-    head_end(1)
-    head_add(6)
     z_step(6, 0)
     z_step(0, 1)
     head_mid(5)
-    head_end(2)
-    head_end(3)
-    head_add(7)
+    head_mid(6)
+    head_mid(7)
+    head_end(0)
+    head_end(1)
     z_step(7, 0)
     z_step(1, 1)
     finish(0)
-    head_mid(6)
+    head_end(2)
+    head_end(3)
+    z_step(2, 1)
     head_end(4)
-    z_step(2, 1)
-    head_mid(7)
     head_end(5)
     z_step(3, 1)
     head_end(6)
@@ -490,7 +518,8 @@
 
             @pl.when(jnp.logical_not((2 * g + w // 2 == d) & (w % 2 == c)))
             def _():
-                slot_copy(g, w).wait_send()
+                slot_copy(g, w, 0).wait_send()
+                slot_copy(g, w, 1).wait_send()
         return carry
 
     lax.fori_loop(0, NB, slots_left, 0)
@@ -529,6 +558,7 @@
     slots = slot_grads[0].transpose(1, 0, 2).reshape(192, 5120)
     rows_in = slot_rows.transpose(2, 0, 1)
     vm = pl.BlockSpec(memory_space=pltpu.VMEM)
+    hbm = pl.BlockSpec(memory_space=pl.ANY)
     dma = pltpu.SemaphoreType.DMA
     grad, table = pl.pallas_call(
         kernel,
@@ -536,9 +566,13 @@
             jax.ShapeDtypeStruct((12, 5120), F32),
             jax.ShapeDtypeStruct((192, 5120), BF16),
         ),
-        in_specs=[vm] * 9,
+        in_specs=[hbm, hbm, vm, hbm, vm, vm, hbm, hbm, hbm],
         out_specs=(vm,) * 2,
         scratch_shapes=[
+            pltpu.VMEM((192, 5120), BF16),
+            pltpu.VMEM((12, 5120), F32),
+            pltpu.VMEM((12, 5120), F32),
+            pltpu.VMEM((12, 5120), F32),
             pltpu.VMEM((32, 160, 1024), BF16),
             pltpu.VMEM((192, 1024), BF16),
             pltpu.VMEM((NB, 4, 64, COLS), BF16),
@@ -559,11 +593,11 @@
             pltpu.VMEM((2, NY, NX, 3, 4, 4 * HALF[0][1]), BF16),
             pltpu.VMEM((2, NY, NX, 3, 4, 4 * HALF[1][1]), BF16),
             dma((2, 9, 2)), dma((2, 9, 2)), dma((2, 9, 2)), dma((2, 9, 2)),
-            dma((32,)), dma((32,)), dma((2, 8, PARTS)), dma((2, 8, PARTS)),
+            dma((2, 32)), dma((2, 32)), dma((2, 8, PARTS)), dma((2, 8, PARTS)),
             dma((NB, 2)), dma((NB, 2)), dma((NB, 2)), dma((NB, 2)), dma((NB, 4)), dma((NB, 4)),
             dma((2, DP)), dma((2, 2, NB)),
             dma((2, 2, 4)), dma((2, 2, 4)), dma((2, 2, 2)), dma((2, 2, 2)), dma((2, 2, 2)), dma((2, 2, 2)),
-            dma((1,)),
+            dma((6,)),
         ],
         compiler_params=pltpu.CompilerParams(
             collective_id=0, has_side_effects=True, vmem_limit_bytes=60 * 1024 * 1024),

time: 157 us -> 153 us (0.975)
  Pallas kernels: 151 us -> 148 us
    pallas_call x1, Pallas kernels: 151 us -> 148 us  [local(): pl.pallas_call(kernel, out_shape=(jax.ShapeDtypeStruct((12, 5120), F32),...]
where the time goes in v3:
time: 153 us
  Pallas kernels  148 us (97%)
  other arithmetic  2.2 us (1%)
    pallas_call x1, Pallas kernels, local(): pl.pallas_call(kernel, out_shape=(jax.ShapeDtypeStruct((12, 5120), F32),...  148 us

profile of v3, /device:TPU:6, one launch (start us, length us, event | category | flops | bytes accessed | tf_op | source)
XLA Modules:
  0.0 152.6 jit_solution(6168147701763545538)
XLA Ops:
  0.6 0.0 copy-start.3
  0.6 0.0 copy-start.2
  0.7 0.0 copy-start.1
  0.7 148.4 %shard_map.120 = (f32[12,5120]{1,0:T(8,128)}, bf16[192,5120]{1,0:T(8,128)(2,1)}) custom-call(bf16[160,1024]{1,0:T(8,128)(2,1)} %bitcast.11, bf16[192,1024]{1,0:T(8,128)(2,1)} %bitcast.10, s32[1,1024]{1,0:T(1,128)} %bitcast.12, bf16[192,5120]{1,0:T(8,128)(2,1)} %bitcast.9, s32[6,1,32]{2,1,0:T(1,128)} %bitcast.13, s32[1,32]{1,0:T(1,128)} %counts.1, ...), custom_call_target="tpu_custom_call" | custom-call | tf_op jit(solution)/shard_map/pallas_call | solution.py:563
  149.0 0.0 copy-start
  149.0 0.0 copy-done.3
  149.1 0.0 copy-done.2
  149.1 0.0 copy-done.1
  149.1 2.2 %multiply_subtract_fusion = (f32[12,5120]{1,0:T(8,128)}, f32[12,5120]{1,0:T(8,128)}, f32[12,5120]{1,0:T(8,128)}) fusion(f32[12,5120]{1,0:T(8,128)S(1)} %copy-done.1, f32[12,5120]{1,0:T(8,128)} %get-tuple-element.6, f32[12,5120]{1,0:T(8,128)S(1)} %copy-done.2, f32[12,5120]{1,0:T(8,128)S(1)} %copy-done.3), kind=kLoop, calls=%fused_computation.2 | loop fusion | flops 921600 | bytes 1720320 | tf_op jit(solution)/shard_map/sub | solution.py:29
  151.3 0.0 copy-done
  151.3 1.3 copy.14
Async XLA Ops:
  0.6 148.4 %copy-start.3 = (f32[12,5120]{1,0:T(8,128)S(1)}, f32[12,5120]{1,0:T(8,128)}, u32[]{:S(2)}) copy-start(f32[12,5120]{1,0:T(8,128)} %second_in.1) | copy-start | bytes 737284
  0.6 148.4 %copy-start.2 = (f32[12,5120]{1,0:T(8,128)S(1)}, f32[12,5120]{1,0:T(8,128)}, u32[]{:S(2)}) copy-start(f32[12,5120]{1,0:T(8,128)} %first_in.1) | copy-start | bytes 737284
  0.7 148.4 %copy-start.1 = (f32[12,5120]{1,0:T(8,128)S(1)}, f32[12,5120]{1,0:T(8,128)}, u32[]{:S(2)}) copy-start(f32[12,5120]{1,0:T(8,128)} %master_in.1) | copy-start | bytes 737284
  149.0 2.2 %copy-start = (bf16[192,5120]{1,0:T(8,128)(2,1)S(1)}, bf16[192,5120]{1,0:T(8,128)(2,1)}, u32[]{:S(2)}) copy-start(bf16[192,5120]{1,0:T(8,128)(2,1)} %get-tuple-element.18) | copy-start | bytes 5898244

commit v4 on v3

--- a/solution.py
+++ b/solution.py
@@ -409,6 +409,61 @@
                     cut = pl.ds(b * n, n)
                     rows = [rowsets[a][w, t // 12, (t // 3) % 4, t % 3, :, cut] for t in units]
                     table[pl.ds(16 * m, 16), pl.ds((4 * w + b) * COLS + off, n)] = jnp.concatenate(rows, axis=0)
+
+    def hidden_left():
+        own_share.wait_send()
+        for s in range(1, 9):
+            for half in (0, 1):
+                for sg in (0, 1):
+                    if s == 8 and half != sg:
+                        continue
+                    ag(sg, s, half).wait_send()
+                    share(sg, s, half).wait_send()
+
+    def slots_left(g, carry):
+        for w in range(4):
+
+            @pl.when(jnp.logical_not((2 * g + w // 2 == d) & (w % 2 == c)))
+            def _():
+                slot_copy(g, w, 0).wait_send()
+                slot_copy(g, w, 1).wait_send()
+        return carry
+
+    def head_left():
+        for n in range(NB):
+            xfirst = n % 2 == 0
+            for side in (0, 1):
+                stage0(n, side, xfirst).wait_send()
+                stage1(n, side, xfirst).wait_send()
+            for o in range(1, 4):
+                stage2(n, ((y if xfirst else x) + o) % 4, xfirst).wait_send()
+
+    def ring_left(a):
+        for s in range(8):
+            for p in range(PARTS):
+                src = part[a].at[0] if s == 0 else ring[a].at[s - 1]
+                if s < 7:
+                    z_copy(s, src, p, a).wait_send()
+                else:
+
+                    @pl.when(c == 0)
+                    def _():
+                        z_copy(s, src, p, a).wait_send()
+
+    def rows_left(a):
+        for t in range(DP):
+
+            @pl.when(jnp.logical_not((t == d) & (h == c)))
+            def _():
+                e_copy(t, a).wait_send()
+
+    def table_left(a):
+        for w in (0, 1):
+            for o in range(1, 4):
+                t1(a, w, (firsts[w] + o) % 4).wait_send()
+            for side in (0, 1):
+                t2(a, w, side).wait_send()
+                t3(a, w, side).wait_send()
 
     own_copy.wait()
     ag_step(1)
@@ -432,13 +487,15 @@
     shares_of(4)
     shares_of(5)
     head_block(3)
+    for n in range(3):
+        head_send(n)
     ag_step(6)
     head_block(4)
+    head_send(3)
+    head_send(4)
     ag_step(7)
     embed_parts(0)
     z_step(0, 0)
-    for n in range(5):
-        head_send(n)
     shares_of(6)
     shares_of(7)
     head_block(5)
@@ -478,6 +535,7 @@
     z_step(7, 0)
     z_step(1, 1)
     finish(0)
+    hidden_left()
     head_end(2)
     head_end(3)
     z_step(2, 1)
@@ -486,6 +544,7 @@
     z_step(3, 1)
     head_end(6)
     head_end(7)
+    lax.fori_loop(0, NB, slots_left, 0)
     z_step(4, 1)
     adam(0)
     spread_rows(0)
@@ -495,63 +554,21 @@
     z_step(7, 1)
     finish(1)
     pass_groups(0)
+    ring_left(0)
+    head_left()
+    adam(1)
+    spread_rows(1)
     gathered(0)
     write_table(0)
-    adam(1)
-    spread_rows(1)
+    rows_left(0)
     spread_groups(1)
+    ring_left(1)
     pass_groups(1)
+    rows_left(1)
+    table_left(0)
     gathered(1)
     write_table(1)
-
-    own_share.wait_send()
-    for s in range(1, 9):
-        for half in (0, 1):
-            for sg in (0, 1):
-                if s == 8 and half != sg:
-                    continue
-                ag(sg, s, half).wait_send()
-                share(sg, s, half).wait_send()
-
-    def slots_left(g, carry):
-        for w in range(4):
-
-            @pl.when(jnp.logical_not((2 * g + w // 2 == d) & (w % 2 == c)))
-            def _():
-                slot_copy(g, w, 0).wait_send()
-                slot_copy(g, w, 1).wait_send()
-        return carry
-
-    lax.fori_loop(0, NB, slots_left, 0)
-    for n in range(NB):
-        xfirst = n % 2 == 0
-        for side in (0, 1):
-            stage0(n, side, xfirst).wait_send()
-            stage1(n, side, xfirst).wait_send()
-        for o in range(1, 4):
-            stage2(n, ((y if xfirst else x) + o) % 4, xfirst).wait_send()
-    for a in (0, 1):
-        for s in range(8):
-            for p in range(PARTS):
-                src = part[a].at[0] if s == 0 else ring[a].at[s - 1]
-                if s < 7:
-                    z_copy(s, src, p, a).wait_send()
-                else:
-
-                    @pl.when(c == 0)
-                    def _():
-                        z_copy(s, src, p, a).wait_send()
-        for t in range(DP):
-
-            @pl.when(jnp.logical_not((t == d) & (h == c)))
-            def _():
-                e_copy(t, a).wait_send()
-        for w in (0, 1):
-            for o in range(1, 4):
-                t1(a, w, (firsts[w] + o) % 4).wait_send()
-            for side in (0, 1):
-                t2(a, w, side).wait_send()
-                t3(a, w, side).wait_send()
+    table_left(1)
 
 
 def local(hidden, logit_grad, predict_mask, slot_grads, slot_rows, slot_counts, master, first, second):

time: 153 us -> 152 us (level)
  no operation moved by 1% of the time
where the time goes in v4:
time: 152 us
  Pallas kernels  148 us (97%)
  other arithmetic  2.2 us (1%)
    pallas_call x1, Pallas kernels, local(): pl.pallas_call(kernel, out_shape=(jax.ShapeDtypeStruct((12, 5120), F32),...  148 us

profile of v4, /device:TPU:6, one launch (start us, length us, event | category | flops | bytes accessed | tf_op | source)
XLA Modules:
  0.0 152.0 jit_solution(4354085770940579935)
XLA Ops:
  0.6 0.0 copy-start.3
  0.6 0.0 copy-start.2
  0.7 0.0 copy-start.1
  0.7 147.8 %shard_map.120 = (f32[12,5120]{1,0:T(8,128)}, bf16[192,5120]{1,0:T(8,128)(2,1)}) custom-call(bf16[160,1024]{1,0:T(8,128)(2,1)} %bitcast.11, bf16[192,1024]{1,0:T(8,128)(2,1)} %bitcast.10, s32[1,1024]{1,0:T(1,128)} %bitcast.12, bf16[192,5120]{1,0:T(8,128)(2,1)} %bitcast.9, s32[6,1,32]{2,1,0:T(1,128)} %bitcast.13, s32[1,32]{1,0:T(1,128)} %counts.1, ...), custom_call_target="tpu_custom_call" | custom-call | tf_op jit(solution)/shard_map/pallas_call | solution.py:580
  148.5 0.0 copy-start
  148.5 0.0 copy-done.3
  148.5 0.0 copy-done.2
  148.5 0.0 copy-done.1
  148.6 2.2 %multiply_subtract_fusion = (f32[12,5120]{1,0:T(8,128)}, f32[12,5120]{1,0:T(8,128)}, f32[12,5120]{1,0:T(8,128)}) fusion(f32[12,5120]{1,0:T(8,128)S(1)} %copy-done.1, f32[12,5120]{1,0:T(8,128)} %get-tuple-element.6, f32[12,5120]{1,0:T(8,128)S(1)} %copy-done.2, f32[12,5120]{1,0:T(8,128)S(1)} %copy-done.3), kind=kLoop, calls=%fused_computation.2 | loop fusion | flops 921600 | bytes 1720320 | tf_op jit(solution)/shard_map/sub | solution.py:29
  150.8 0.0 copy-done
  150.8 1.3 copy.14
Async XLA Ops:
  0.6 147.9 %copy-start.3 = (f32[12,5120]{1,0:T(8,128)S(1)}, f32[12,5120]{1,0:T(8,128)}, u32[]{:S(2)}) copy-start(f32[12,5120]{1,0:T(8,128)} %second_in.1) | copy-start | bytes 737284
  0.6 147.9 %copy-start.2 = (f32[12,5120]{1,0:T(8,128)S(1)}, f32[12,5120]{1,0:T(8,128)}, u32[]{:S(2)}) copy-start(f32[12,5120]{1,0:T(8,128)} %first_in.1) | copy-start | bytes 737284
  0.7 147.9 %copy-start.1 = (f32[12,5120]{1,0:T(8,128)S(1)}, f32[12,5120]{1,0:T(8,128)}, u32[]{:S(2)}) copy-start(f32[12,5120]{1,0:T(8,128)} %master_in.1) | copy-start | bytes 737284
  148.5 2.2 %copy-start = (bf16[192,5120]{1,0:T(8,128)(2,1)S(1)}, bf16[192,5120]{1,0:T(8,128)(2,1)}, u32[]{:S(2)}) copy-start(bf16[192,5120]{1,0:T(8,128)(2,1)} %get-tuple-element.18) | copy-start | bytes 5898244
